TPU v7x, 32 devices: a whole 2x2x4 slice. The times are simulated.
32 devices in a mesh: dp: 4 (over z), seq: 8 (over y, x, core).
Axes of the slice: x: 2, y: 2, z: 4, core: 2. Of those that a mesh axis runs over, the one named last changes fastest.
Arguments:
- inputs: bfloat16 [4, 65536, 512], P('dp', 'seq'), may hold values from -6 to 6
- cotangent: bfloat16 [4, 65536, 512], P('dp', 'seq'), may hold values from -6 to 6
- value_weight: bfloat16 [512, 512], replicated, may hold values from -0.25 to 0.25
- gate_weight: bfloat16 [512, 512], replicated, may hold values from -0.25 to 0.25
- first_blocks: bfloat16 [256, 256, 256], P('seq'), may hold values from -0.375 to 0.375
- second_blocks: bfloat16 [256, 256, 256], P('seq'), may hold values from -0.375 to 0.375
Outputs:
- grad_inputs: bfloat16 [4, 65536, 512], P('dp', 'seq')
- grad_value_weight: float32 [512, 512], replicated
- grad_gate_weight: float32 [512, 512], replicated
- grad_first_blocks: float32 [256, 256, 256], P('seq')
- grad_second_blocks: float32 [256, 256, 256], P('seq')
All inputs are finite; a program needn't handle non-finite values.
Results may differ from a plain program's by a relative error of at most 0.014.
Values may be sent and summed in bfloat16 or wider, within the bound.
A program may use at most 256 MiB of HBM per device.

v0:
```python
import jax
import jax.numpy as jnp
from jax import lax
from jax.sharding import PartitionSpec as P


def on_device(inputs, cotangent, value_weight, gate_weight, first_blocks, second_blocks):
    groups, own_tokens, channels = inputs.shape
    own_blocks, block_len, _ = first_blocks.shape
    flat_in = inputs.reshape(groups * own_tokens, channels)
    cot_flat = cotangent.reshape(groups * own_tokens, channels)
    values = jnp.dot(flat_in, value_weight, preferred_element_type=jnp.float32).astype(jnp.bfloat16)
    gate_rows = jnp.dot(flat_in, gate_weight, preferred_element_type=jnp.float32).astype(
        jnp.bfloat16
    )
    value_blk = values.reshape(groups, own_blocks, block_len, channels)
    first_mix = jnp.einsum(
        "aqp,sapd->saqd", first_blocks, value_blk, preferred_element_type=jnp.float32
    ).astype(jnp.bfloat16)
    spread_mix = lax.all_to_all(first_mix, "seq", split_axis=2, concat_axis=1, tiled=True)
    second_mix = lax.all_to_all(
        jnp.einsum(
            "pba,sapd->sbpd", second_blocks, spread_mix, preferred_element_type=jnp.float32
        ).astype(jnp.bfloat16),
        "seq",
        split_axis=1,
        concat_axis=2,
        tiled=True,
    )
    grad_mix = (cot_flat.astype(jnp.float32) * gate_rows.astype(jnp.float32)).astype(jnp.bfloat16)
    spread_grad = lax.all_to_all(
        grad_mix.reshape(groups, own_blocks, block_len, channels),
        "seq",
        split_axis=2,
        concat_axis=1,
        tiled=True,
    )
    grad_first_mix = lax.all_to_all(
        jnp.einsum(
            "pba,sbpd->sapd", second_blocks, spread_grad, preferred_element_type=jnp.float32
        ).astype(jnp.bfloat16),
        "seq",
        split_axis=1,
        concat_axis=2,
        tiled=True,
    )
    grad_second = jnp.einsum(
        "sbpd,sapd->pba", spread_grad, spread_mix, preferred_element_type=jnp.float32
    )
    grad_gates = (
        cot_flat.astype(jnp.float32)
        * second_mix.reshape(groups * own_tokens, channels).astype(jnp.float32)
    ).astype(jnp.bfloat16)
    grad_values = jnp.einsum(
        "aqp,saqd->sapd", first_blocks, grad_first_mix, preferred_element_type=jnp.float32
    ).astype(jnp.bfloat16)
    grad_first = jnp.einsum(
        "saqd,sapd->aqp", grad_first_mix, value_blk, preferred_element_type=jnp.float32
    )
    flat_gv = grad_values.reshape(groups * own_tokens, channels)
    contract = (((0,), (0,)), ((), ()))
    w_val = lax.dot_general(flat_in, flat_gv, contract, preferred_element_type=jnp.float32)
    w_gate = lax.dot_general(flat_in, grad_gates, contract, preferred_element_type=jnp.float32)
    backward = (((1,), (1,)), ((), ()))
    grad_in = (
        lax.dot_general(flat_gv, value_weight, backward, preferred_element_type=jnp.float32)
        + lax.dot_general(grad_gates, gate_weight, backward, preferred_element_type=jnp.float32)
    ).astype(jnp.bfloat16)
    w_val, w_gate = lax.psum((w_val, w_gate), ("dp", "seq"))
    grad_first, grad_second = lax.psum((grad_first, grad_second), "dp")
    total_rows = groups * lax.axis_size("dp") * own_tokens * lax.axis_size("seq")
    weight_scale = 1.0 / jnp.sqrt(jnp.float32(total_rows))
    block_scale = 1.0 / jnp.sqrt(jnp.float32(groups * lax.axis_size("dp") * channels))
    return (
        grad_in.reshape(inputs.shape),
        w_val * weight_scale,
        w_gate * weight_scale,
        grad_first * block_scale,
        grad_second * block_scale,
    )


def solution(mesh):
    placed = (
        P("dp", "seq", None),
        P("dp", "seq", None),
        P(),
        P(),
        P("seq", None, None),
        P("seq", None, None),
    )
    return jax.shard_map(
        on_device,
        mesh=mesh,
        in_specs=placed,
        out_specs=(P("dp", "seq", None), P(), P(), P("seq", None, None), P("seq", None, None)),
        check_vma=False,
    )
```

profile of v0, /device:TPU:0, one launch (start us, length us, event | category | flops | bytes accessed | tf_op | source)
XLA Modules:
  0.0 1183.3 jit_solution(2482332922046529265)
XLA Ops:
  7.2 0.0 copy-start
  7.2 1.0 copy-done
  8.2 8.1 convolution_convert_fusion
  16.3 3.3 copy-done.3
  19.6 8.2 convert_bitcast_fusion.3
  27.8 14.5 %copy.60 = bf16[1,32,256,512]{3,1,0,2:T(8,128)(2,1)} copy(bf16[1,32,256,512]{2,3,1,0:T(8,128)(2,1)} %convert_bitcast_fusion.3) | data formatting | bytes 16777216 | tf_op jit(solution)/shard_map/convert_element_type | solution.py:19
  42.3 5.5 all-to-all-start.2
  47.8 11.4 fusion.2
  59.3 11.5 copy.52
  70.8 71.5 %all-to-all-done.2 = bf16[1,32,256,512]{3,1,0,2:T(8,128)(2,1)} async-done(((bf16[1,32,256,512]{3,1,0,2:T(8,128)(2,1)}), bf16[1,32,256,512]{3,1,0,2:T(8,128)(2,1)}, u32[]{:S(2)}, u32[]{:S(2)}) %all-to-all-start.2) | async-done | bytes 8388640 | tf_op jit(solution)/shard_map/all_to_all | solution.py:20
  142.3 5.2 all-to-all-start
  147.5 11.5 copy.61
  159.0 8.4 copy.62
  167.4 41.3 %convert_bitcast_fusion.2 = bf16[1,256,32,512]{1,3,2,0:T(8,128)(2,1)} fusion(bf16[32,256,256]{2,1,0:T(8,128)(2,1)S(1)} %copy-done.4, bf16[256,32,512]{2,1,0:T(8,128)(2,1)} %bitcast.102), kind=kOutput, calls=%fused_computation.19 | convolution fusion | flops 2151677952 | bytes 20971520 | tf_op jit(solution)/shard_map/pba,sapd->sbpd/dot_general | solution.py:22
  208.8 14.7 %copy.64 = bf16[1,256,32,512]{3,2,0,1:T(8,128)(2,1)} copy(bf16[1,256,32,512]{1,3,2,0:T(8,128)(2,1)} %convert_bitcast_fusion.2) | data formatting | bytes 16777216 | tf_op jit(solution)/shard_map/convert_element_type | solution.py:24
  223.5 18.1 %all-to-all-done = bf16[1,32,256,512]{3,1,0,2:T(8,128)(2,1)} async-done(((bf16[1,32,256,512]{3,1,0,2:T(8,128)(2,1)}), bf16[1,32,256,512]{3,1,0,2:T(8,128)(2,1)}, u32[]{:S(2)}, u32[]{:S(2)}) %all-to-all-start) | async-done | bytes 8388640 | tf_op jit(solution)/shard_map/all_to_all | solution.py:31
  241.6 4.9 all-to-all-start.3
  246.5 11.5 copy.53
  258.0 8.6 copy.54
  266.6 16.7 %convert_bitcast_fusion.4 = bf16[1,256,32,512]{1,3,2,0:T(8,128)(2,1)} fusion(bf16[32,256,256]{2,1,0:T(8,128)(2,1)S(1)} %copy-done.5, bf16[256,32,512]{2,1,0:T(8,128)(2,1)} %bitcast.92), kind=kOutput, calls=%fused_computation.21 | convolution fusion | flops 2151677952 | bytes 20971520 | tf_op jit(solution)/shard_map/pba,sbpd->sapd/dot_general | solution.py:39
  283.3 14.5 %copy.56 = bf16[1,256,32,512]{3,2,0,1:T(8,128)(2,1)} copy(bf16[1,256,32,512]{1,3,2,0:T(8,128)(2,1)} %convert_bitcast_fusion.4) | data formatting | bytes 16777216 | tf_op jit(solution)/shard_map/convert_element_type | solution.py:41
  297.9 42.7 %all-to-all-done.3 = bf16[1,256,32,512]{3,2,0,1:T(8,128)(2,1)} async-done(((bf16[1,256,32,512]{3,2,0,1:T(8,128)(2,1)}), bf16[1,256,32,512]{3,2,0,1:T(8,128)(2,1)}, u32[]{:S(2)}, u32[]{:S(2)}) %all-to-all-start.3) | async-done | bytes 8388640 | tf_op jit(solution)/shard_map/all_to_all | solution.py:21
  340.6 5.0 all-to-all-start.1
  345.6 0.0 all-reduce.5.cloned.1.call-start
  345.6 11.7 convert_bitcast_fusion.1
  357.3 7.2 copy.66
  364.5 8.1 fusion.4
  372.7 1.0 copy-done.1
  373.7 11.2 fusion.24
  384.9 54.7 %all-to-all-done.1 = bf16[1,256,32,512]{3,2,0,1:T(8,128)(2,1)} async-done(((bf16[1,256,32,512]{3,2,0,1:T(8,128)(2,1)}), bf16[1,256,32,512]{3,2,0,1:T(8,128)(2,1)}, u32[]{:S(2)}, u32[]{:S(2)}) %all-to-all-start.1) | async-done | bytes 8388640 | tf_op jit(solution)/shard_map/all_to_all | solution.py:38
  439.6 8.4 copy.57
  448.1 6.1 convolution_convert_fusion.2
  454.2 3.4 copy-done.2
  457.6 7.9 fusion.29
  465.5 0.0 all-reduce.5.cloned.1.call-update
  465.5 0.4 all-reduce.7.cloned.1.call-start
  466.0 18.2 %fusion.15 = f32[32,256,256]{2,1,0:T(8,128)} fusion(bf16[256,32,512]{2,1,0:T(8,128)(2,1)} %bitcast.103, bf16[256,32,512]{2,1,0:T(8,128)(2,1)} %bitcast.93), kind=kOutput, calls=%fused_computation.24 | convolution fusion | flops 2147483648 | bytes 25165824 | tf_op jit(solution)/shard_map/sbpd,sapd->pba/dot_general | solution.py:47
  484.2 11.6 fusion.33
  495.8 0.0 all-reduce.7.cloned.1.call-update
  495.8 11.9 %fusion.32 = f32[8192,512]{1,0:T(8,128)} fusion(bf16[8192,512]{1,0:T(8,128)(2,1)} %bitcast.95, bf16[512,512]{1,0:T(8,128)(2,1)S(1)} %copy-done), kind=kOutput, calls=%fused_computation.36 | convolution fusion | flops 4294967296 | bytes 25690112 | tf_op jit(solution)/shard_map/dot_general | solution.py:66
  507.8 12.1 %fusion.3 = bf16[8192,512]{1,0:T(8,128)(2,1)} fusion(bf16[1,8192,512]{2,1,0:T(8,128)(2,1)} %param.7, f32[1,32,8,32,512]{4,3,2,1,0:T(8,128)} %copy-done.1), kind=kLoop, calls=%fused_computation.5 | loop fusion | flops 12582912 | bytes 33554432 | tf_op jit(solution)/shard_map/convert_element_type | solution.py:53
  519.9 12.6 %fusion.5 = bf16[1,8192,512]{2,1,0:T(8,128)(2,1)} fusion(f32[8192,512]{1,0:T(8,128)} %fusion.32, bf16[8192,512]{1,0:T(8,128)(2,1)} %fusion.3, bf16[512,512]{1,0:T(8,128)(2,1)S(1)} %copy-done.7), kind=kOutput, calls=%fused_computation.11 | convolution fusion | flops 4303355904 | bytes 34078720 | tf_op jit(solution)/shard_map/dot_general | solution.py:67
  532.5 67.5 %all-reduce.5.cloned.1.call-done = (f32[512,512]{0,1:T(8,128)}, f32[512,512]{0,1:T(8,128)}) async-done(((f32[512,512]{0,1:T(8,128)}, f32[512,512]{0,1:T(8,128)}), (f32[512,512]{0,1:T(8,128)}, f32[512,512]{0,1:T(8,128)})) %all-reduce.5.cloned.1.call-update) | async-done | bytes 2097168 | tf_op jit(solution)/shard_map/psum | solution.py:69
  600.0 1.8 broadcast_multiply_fusion.2
  601.8 1.3 copy.71
  603.1 1.3 copy.70
  604.4 561.1 %all-reduce.7.cloned.1.call-done = (f32[32,256,256]{2,1,0:T(8,128)}, f32[32,256,256]{2,1,0:T(8,128)}) async-done(((f32[32,256,256]{2,1,0:T(8,128)}, f32[32,256,256]{2,1,0:T(8,128)}), (f32[32,256,256]{2,1,0:T(8,128)}, f32[32,256,256]{2,1,0:T(8,128)})) %all-reduce.7.cloned.1.call-update) | async-done | bytes 16777232 | tf_op jit(solution)/shard_map/psum | solution.py:70
  1165.6 10.7 broadcast_multiply_fusion
  (16 shorter events, 0.0 us)
Async XLA Ops:
  7.2 1.0 copy-start
  16.3 3.3 copy-start.3
  42.3 5.5 copy-start.6
  42.3 100.0 %all-to-all-start.2 = ((bf16[1,32,256,512]{3,1,0,2:T(8,128)(2,1)}), bf16[1,32,256,512]{3,1,0,2:T(8,128)(2,1)}, u32[]{:S(2)}, u32[]{:S(2)}) async-start(bf16[1,32,256,512]{3,1,0,2:T(8,128)(2,1)} %copy.60), calls=%async_computation.2 | async-start | bytes 16777216 | tf_op jit(solution)/shard_map/all_to_all | solution.py:20
  142.3 99.3 %all-to-all-start = ((bf16[1,32,256,512]{3,1,0,2:T(8,128)(2,1)}), bf16[1,32,256,512]{3,1,0,2:T(8,128)(2,1)}, u32[]{:S(2)}, u32[]{:S(2)}) async-start(bf16[1,32,256,512]{3,1,0,2:T(8,128)(2,1)} %copy.52), calls=%async_computation | async-start | bytes 16777216 | tf_op jit(solution)/shard_map/all_to_all | solution.py:31
  159.0 8.4 copy-start.4
  241.6 99.0 %all-to-all-start.3 = ((bf16[1,256,32,512]{3,2,0,1:T(8,128)(2,1)}), bf16[1,256,32,512]{3,2,0,1:T(8,128)(2,1)}, u32[]{:S(2)}, u32[]{:S(2)}) async-start(bf16[1,256,32,512]{3,2,0,1:T(8,128)(2,1)} %copy.64), calls=%async_computation.3 | async-start | bytes 16777216 | tf_op jit(solution)/shard_map/all_to_all | solution.py:21
  258.0 8.6 copy-start.5
  340.6 99.0 %all-to-all-start.1 = ((bf16[1,256,32,512]{3,2,0,1:T(8,128)(2,1)}), bf16[1,256,32,512]{3,2,0,1:T(8,128)(2,1)}, u32[]{:S(2)}, u32[]{:S(2)}) async-start(bf16[1,256,32,512]{3,2,0,1:T(8,128)(2,1)} %copy.56), calls=%async_computation.1 | async-start | bytes 16777216 | tf_op jit(solution)/shard_map/all_to_all | solution.py:38
  345.6 254.4 %all-reduce.5.cloned.1.call-start = ((), (), s32[]{:S(2)}) async-start(), calls=%async_computation.4 | async-start | bytes 4194304 | tf_op jit(solution)/shard_map/psum | solution.py:69
  345.6 18.9 %slice-start = ((s8[8388608]{0:T(1024)(128)(4,1)}), s8[4194304]{0:T(1024)(128)(4,1)S(1)}, s32[]{:S(2)}) async-start(s8[8388608]{0:T(1024)(128)(4,1)} %bitcast.100), calls=%async_computation.6 | async-start | bytes 8388608
  357.3 7.2 slice-start.1
  364.5 9.2 copy-start.1
  454.2 3.4 copy-start.2
  465.5 700.1 %all-reduce.7.cloned.1.call-start = ((), (), s32[]{:S(2)}) async-start(), calls=%async_computation.5 | async-start | bytes 33554432 | tf_op jit(solution)/shard_map/psum | solution.py:70
  507.8 12.1 %copy-start.7 = (bf16[512,512]{1,0:T(8,128)(2,1)S(1)}, bf16[512,512]{1,0:T(8,128)(2,1)}, u32[]{:S(2)}) copy-start(bf16[512,512]{1,0:T(8,128)(2,1)} %param.9) | copy-start | bytes 1572868
Sparse Core Ops, SparseCore 0:
  465.6 134.3 all-reduce.4
  603.4 562.1 all-reduce.6
where the time goes:
time: 1190 us; the launch traced here: 1180 us
  waiting for transfers between devices  816 us (69%)
  matrix products  165 us (14%)
  local copies, waits for them, and re-layouts  122 us (10%)
  other arithmetic  44.4 us (4%)
  starting transfers between devices  21.1 us (2%)
  between operations  14.4 us (1%)
    psum x1, waiting for transfers between devices, on_device(): grad_first, grad_second = lax.psum((grad_first, grad_second), 'dp')  561 us
    all_to_all x1, waiting for transfers between devices, on_device(): lax.all_to_all(first_mix, 'seq', split_axis=2, concat_axis=1, tiled=True)  71.5 us
    psum x1, waiting for transfers between devices, on_device(): w_val, w_gate = lax.psum((w_val, w_gate), ('dp', 'seq'))  67.5 us
    all_to_all x1, waiting for transfers between devices, on_device(): lax.all_to_all(jnp.einsum('pba,sbpd->sapd', second_blocks, spread_grad, p...  54.7 us
    all_to_all x1, waiting for transfers between devices, on_device(): lax.all_to_all(jnp.einsum('pba,sapd->sbpd', second_blocks, spread_mix, pr...  42.7 us
    dot_general x1, matrix products, on_device(): jnp.einsum('pba,sapd->sbpd', second_blocks, spread_mix, preferred_element...  41.3 us
  transfers between devices with their start and end apart: 6, of which 6 were waited for; matrix products, arithmetic and copies ran while one was open for 22% of the time, Pallas kernels for 0%

commit v1 on v0

v1 whole, which is shorter than its diff:
```python
import jax
import jax.numpy as jnp
from jax import lax
from jax.experimental import pallas as pl
from jax.sharding import PartitionSpec as P

BF = jnp.bfloat16
F32 = jnp.float32


def packed_grad_mix(x, cot, weight, blocks, n):
    rows, channels = x.shape
    length = rows // blocks
    own = length // n

    def body(x_ref, c_ref, w_ref, o_ref):
        gate = jnp.dot(x_ref[...], w_ref[...], preferred_element_type=F32).astype(BF)
        mix = (c_ref[...].astype(F32) * gate.astype(F32)).astype(BF)
        o_ref[...] = mix.reshape(n, 1, own, channels)

    return pl.pallas_call(
        body,
        out_shape=jax.ShapeDtypeStruct((n, blocks, own, channels), BF),
        grid=(blocks,),
        in_specs=[
            pl.BlockSpec((length, channels), lambda a: (a, 0)),
            pl.BlockSpec((length, channels), lambda a: (a, 0)),
            pl.BlockSpec((channels, channels), lambda a: (0, 0)),
        ],
        out_specs=pl.BlockSpec((n, 1, own, channels), lambda a: (0, a, 0, 0)),
        cost_estimate=pl.CostEstimate(
            flops=2 * rows * channels * channels, bytes_accessed=6 * rows * channels, transcendentals=0
        ),
    )(x, cot, weight)


def packed_first_mix(factor, values, order, n):
    blocks, length, channels = values.shape
    own = length // n

    def body(f_ref, v_ref, _, o_ref):
        mix = jnp.dot(f_ref[0], v_ref[0], preferred_element_type=F32).astype(BF)
        o_ref[...] = mix.reshape(n, 1, own, channels)

    return pl.pallas_call(
        body,
        out_shape=jax.ShapeDtypeStruct((n, blocks, own, channels), BF),
        grid=(blocks,),
        in_specs=[
            pl.BlockSpec((1, length, length), lambda a: (a, 0, 0)),
            pl.BlockSpec((1, length, channels), lambda a: (a, 0, 0)),
            pl.BlockSpec(memory_space=pl.ANY),
        ],
        out_specs=pl.BlockSpec((n, 1, own, channels), lambda a: (0, a, 0, 0)),
        cost_estimate=pl.CostEstimate(
            flops=2 * blocks * length * length * channels,
            bytes_accessed=5 * blocks * length * channels,
            transcendentals=0,
        ),
    )(factor, values, order)


def nought(x):
    return jnp.minimum(jnp.abs(x[(0,) * x.ndim]), 0).astype(x.dtype)


def dp_sum(x):
    n = lax.axis_size("dp")
    me = lax.axis_index("dp")
    parts = x.reshape((n, x.shape[0] // n) + x.shape[1:])

    def shift(v, by):
        return lax.ppermute(v, "dp", [(i, (i + by) % n) for i in range(n)])

    total = lax.dynamic_index_in_dim(parts, me, 0, keepdims=False).astype(F32)
    got = [
        shift(lax.dynamic_index_in_dim(parts, (me + by) % n, 0, keepdims=False), by)
        for by in range(1, n)
    ]
    for g in got:
        total = total + g.astype(F32)
    total = total.astype(BF)
    out = jnp.zeros(parts.shape, F32)
    out = lax.dynamic_update_index_in_dim(out, total.astype(F32), me, 0)
    for by in range(1, n):
        out = lax.dynamic_update_index_in_dim(
            out, shift(total, by).astype(F32), (me - by + n) % n, 0
        )
    return out.reshape(x.shape), total


def whole_sum(x):
    n = lax.axis_size("seq")
    rows = lax.all_to_all(
        x.reshape((n, x.shape[0] // n) + x.shape[1:]), "seq", split_axis=0, concat_axis=0, tiled=True
    )
    mine = jnp.sum(rows, axis=0)
    mine = jnp.sum(lax.all_gather(mine, "dp"), axis=0)
    return lax.all_gather(mine, "seq", tiled=True)


def on_device(inputs, cotangent, value_weight, gate_weight, first_blocks, second_blocks):
    groups, own_tokens, channels = inputs.shape
    own_blocks, block_len, _ = first_blocks.shape
    n_seq = lax.axis_size("seq")
    own_p = block_len // n_seq
    rows = groups * own_tokens
    flat_in = inputs.reshape(rows, channels)
    cot_flat = cotangent.reshape(rows, channels)

    def exchange(x):
        return lax.all_to_all(x, "seq", split_axis=0, concat_axis=0, tiled=True)

    def to_p(x):
        return exchange(x).reshape(-1, own_p, channels)

    def to_a(x):
        got = exchange(x.reshape(n_seq, own_blocks, own_p, channels))
        return got.transpose(1, 0, 2, 3).reshape(own_blocks, block_len, channels)

    grad_mix = packed_grad_mix(flat_in, cot_flat, gate_weight, own_blocks, n_seq)
    spread_grad = to_p(grad_mix)

    values = jnp.dot(flat_in, value_weight, preferred_element_type=F32).astype(BF)
    value_blk = values.reshape(own_blocks, block_len, channels)
    spread_mix = to_p(packed_first_mix(first_blocks, value_blk, spread_grad, n_seq))

    gfm = jnp.einsum("pba,bpd->apd", second_blocks, spread_grad, preferred_element_type=F32)
    grad_first_mix = to_a(gfm.astype(BF))

    total_rows = rows * lax.axis_size("dp") * n_seq
    weight_scale = 1.0 / jnp.sqrt(F32(total_rows))
    block_scale = 1.0 / jnp.sqrt(F32(lax.axis_size("dp") * channels))

    grad_second = jnp.einsum("bpd,apd->pba", spread_grad, spread_mix, preferred_element_type=F32)
    grad_second = (grad_second * block_scale).astype(BF)
    smix = jnp.einsum("pba,apd->bpd", second_blocks + nought(grad_second), spread_mix, preferred_element_type=F32)
    second_mix = to_a(smix.astype(BF))
    grad_second = lax.psum(grad_second, "dp")

    grad_first = jnp.einsum("aqd,apd->aqp", grad_first_mix, value_blk, preferred_element_type=F32)
    grad_first = (grad_first * block_scale).astype(BF)
    grad_first, share = dp_sum(grad_first)
    later = nought(share).astype(F32)

    grad_values = jnp.einsum(
        "aqp,aqd->apd", first_blocks, grad_first_mix, preferred_element_type=F32
    ).astype(BF)
    flat_gv = grad_values.reshape(rows, channels)
    contract = (((0,), (0,)), ((), ()))
    backward = (((1,), (1,)), ((), ()))
    w_val = lax.dot_general(flat_in, flat_gv, contract, preferred_element_type=F32)

    grad_gates = (cot_flat.astype(F32) * (second_mix.reshape(rows, channels).astype(F32) + later)).astype(BF)
    w_gate = lax.dot_general(flat_in, grad_gates, contract, preferred_element_type=F32)
    w_val, w_gate = jnp.split(whole_sum(jnp.concatenate([w_val, w_gate]) * weight_scale), 2)
    grad_in = (
        lax.dot_general(flat_gv, value_weight, backward, preferred_element_type=F32)
        + lax.dot_general(grad_gates, gate_weight, backward, preferred_element_type=F32)
    ).astype(BF)
    return (
        grad_in.reshape(inputs.shape),
        w_val,
        w_gate,
        grad_first,
        grad_second.astype(F32),
    )


def solution(mesh):
    placed = (
        P("dp", "seq", None),
        P("dp", "seq", None),
        P(),
        P(),
        P("seq", None, None),
        P("seq", None, None),
    )
    return jax.shard_map(
        on_device,
        mesh=mesh,
        in_specs=placed,
        out_specs=(P("dp", "seq", None), P(), P(), P("seq", None, None), P("seq", None, None)),
        check_vma=False,
    )
```

time: 1190 us -> 767 us (0.64)
  waiting for transfers between devices: 816 us -> 388 us
  local copies, waits for them, and re-layouts: 122 us -> 45.9 us
  starting transfers between devices: 21.1 us -> 84.2 us
  Pallas kernels: 0 us -> 48.5 us
  matrix products: 165 us -> 128 us
    psum x2 -> x1, waiting for transfers between devices: 629 us -> 0.01 us  [on_device(): grad_second = lax.psum(grad_second, 'dp')]
    ppermute x0 -> x6, waiting for transfers between devices: none -> 166 us  [shift(): return lax.ppermute(v, 'dp', [(i, (i + by) % n) for i in range(n)])]
    ppermute x0 -> x6, starting transfers between devices: none -> 60.2 us  [shift(): return lax.ppermute(v, 'dp', [(i, (i + by) % n) for i in range(n)])]
    convert_element_type x4 -> x0, local copies, waits for them, and re-layouts: 50.9 us -> none  [the longest x1 14.7 us: on_device(): second_mix = lax.all_to_all(jnp.einsum('pba,sapd->sbpd', second_blocks, s...]
    all_to_all x5 -> x0, local copies, waits for them, and re-layouts: 48.5 us -> none  [the longest x2 20.1 us: on_device(): lax.all_to_all(grad_mix.reshape(groups, own_blocks, block_len, channels),...]
    pallas_call x0 -> x2, Pallas kernels: none -> 48.5 us  [the longest x1 25.1 us: packed_grad_mix(): pl.pallas_call(body, out_shape=jax.ShapeDtypeStruct((n, blocks, own, chan...]
    dot_general x11 -> x9, matrix products: 153 us -> 115 us  [the longest x1 18.3 us: on_device(): jnp.einsum('pba,apd->bpd', second_blocks + nought(grad_second), spread_mi...]
    all_gather x0 -> x2, waiting for transfers between devices: none -> 23.2 us  [the longest x1 23.2 us: whole_sum(): return lax.all_gather(mine, 'seq', tiled=True)]
  transfers between devices with their start and end apart: 6 -> 14, of which waited for: 6 -> 8; matrix products, arithmetic and copies ran while one was open for 22% -> 28% of each run, Pallas kernels for 0% -> 0%
where the time goes in v1:
time: 767 us; the launch traced here: 758 us
  waiting for transfers between devices  388 us (51%)
  matrix products  128 us (17%)
  starting transfers between devices  84.2 us (11%)
  Pallas kernels  48.5 us (6%)
  other arithmetic  47.8 us (6%)
  local copies, waits for them, and re-layouts  45.9 us (6%)
  between operations  15.7 us (2%)
    all_to_all x4, waiting for transfers between devices, exchange(): return lax.all_to_all(x, 'seq', split_axis=0, concat_axis=0, tiled=True)  198 us
    ppermute x6, waiting for transfers between devices, shift(): return lax.ppermute(v, 'dp', [(i, (i + by) % n) for i in range(n)])  166 us
    ppermute x6, starting transfers between devices, shift(): return lax.ppermute(v, 'dp', [(i, (i + by) % n) for i in range(n)])  60.2 us
    pallas_call x1, Pallas kernels, packed_grad_mix(): pl.pallas_call(body, out_shape=jax.ShapeDtypeStruct((n, blocks, own, chan...  25.1 us
    pallas_call x1, Pallas kernels, packed_first_mix(): pl.pallas_call(body, out_shape=jax.ShapeDtypeStruct((n, blocks, own, chan...  23.4 us
    all_gather x1, waiting for transfers between devices, whole_sum(): return lax.all_gather(mine, 'seq', tiled=True)  23.2 us
    reshape x2, local copies, waits for them, and re-layouts, to_a(): got = exchange(x.reshape(n_seq, own_blocks, own_p, channels))  20.5 us
    all_to_all x4, starting transfers between devices, exchange(): return lax.all_to_all(x, 'seq', split_axis=0, concat_axis=0, tiled=True)  20.3 us
  transfers between devices with their start and end apart: 14, of which 8 were waited for; matrix products, arithmetic and copies ran while one was open for 28% of the time, Pallas kernels for 0%

profile of v1, /device:TPU:0, one launch (start us, length us, event | category | flops | bytes accessed | tf_op | source)
XLA Modules:
  0.0 757.6 jit_solution(17292950934116374751)
XLA Ops:
  7.2 25.1 %shard_map.101 = bf16[8,32,32,512]{3,2,1,0:T(8,128)(2,1)} custom-call(bf16[8192,512]{1,0:T(8,128)(2,1)} %bitcast.87, bf16[8192,512]{1,0:T(8,128)(2,1)} %bitcast.83, bf16[512,512]{1,0:T(8,128)(2,1)} %w_ref.1), custom_call_target="tpu_custom_call" | custom-call | flops 4294967296 | bytes 25165824 | tf_op jit(solution)/shard_map/pallas_call | solution.py:21
  32.3 5.2 all-to-all-start
  37.5 10.1 %convolution_convert_fusion = bf16[8192,512]{1,0:T(8,128)(2,1)} fusion(bf16[512,512]{1,0:T(8,128)(2,1)S(1)} %copy-done, bf16[1,8192,512]{2,1,0:T(8,128)(2,1)} %param.6), kind=kOutput, calls=%fused_computation.5 | convolution fusion | flops 4299161600 | bytes 17301504 | tf_op jit(solution)/shard_map/dot_general | solution.py:124
  47.6 84.4 %all-to-all-done = bf16[8,32,32,512]{3,2,1,0:T(8,128)(2,1)} async-done(((bf16[8,32,32,512]{3,2,1,0:T(8,128)(2,1)}), bf16[8,32,32,512]{3,2,1,0:T(8,128)(2,1)}, u32[]{:S(2)}, u32[]{:S(2)}) %all-to-all-start) | async-done | bytes 8388640 | tf_op jit(solution)/shard_map/all_to_all | solution.py:112
  132.0 23.4 %shard_map.102 = bf16[8,32,32,512]{3,2,1,0:T(8,128)(2,1)} custom-call(bf16[32,256,256]{2,1,0:T(8,128)(2,1)} %f_ref.1, bf16[32,256,512]{2,1,0:T(8,128)(2,1)} %bitcast.91, bf16[256,32,512]{2,1,0:T(8,128)(2,1)} %bitcast.2._), custom_call_target="tpu_custom_call" | custom-call | flops 2147483648 | bytes 20971520 | tf_op jit(solution)/shard_map/pallas_call | solution.py:45
  155.4 5.0 all-to-all-start.2
  160.4 16.4 %fusion.12 = bf16[32,512,256]{1,2,0:T(8,128)(2,1)} fusion(bf16[32,256,256]{2,1,0:T(8,128)(2,1)} %param.11, bf16[256,32,512]{2,1,0:T(8,128)(2,1)} %bitcast.2._), kind=kOutput, calls=%fused_computation.18 | convolution fusion | flops 2151677952 | bytes 20971520 | tf_op jit(solution)/shard_map/pba,bpd->apd/dot_general | solution.py:128
  176.8 8.4 %copy.41 = bf16[8,32,32,512]{3,1,2,0:T(8,128)(2,1)} copy(bf16[8,32,32,512]{3,1,0,2:T(8,128)(2,1)} %bitcast.84) | data formatting | bytes 16777216 | tf_op jit(solution)/shard_map/reshape | solution.py:118
  185.2 69.3 %all-to-all-done.2 = bf16[8,32,32,512]{3,2,1,0:T(8,128)(2,1)} async-done(((bf16[8,32,32,512]{3,2,1,0:T(8,128)(2,1)}), bf16[8,32,32,512]{3,2,1,0:T(8,128)(2,1)}, u32[]{:S(2)}, u32[]{:S(2)}) %all-to-all-start.2) | async-done | bytes 8388640 | tf_op jit(solution)/shard_map/all_to_all | solution.py:112
  254.5 5.2 all-to-all-start.1
  259.7 17.3 %multiply_convert_fusion.2 = bf16[32,256,256]{2,1,0:T(8,128)(2,1)} fusion(bf16[256,32,512]{2,1,0:T(8,128)(2,1)} %bitcast.10, bf16[256,32,512]{2,1,0:T(8,128)(2,1)} %bitcast.2._), kind=kOutput, calls=%fused_computation.10 | convolution fusion | flops 2151677952 | bytes 20971520 | tf_op jit(solution)/shard_map/bpd,apd->pba/dot_general | solution.py:135
  277.0 1.2 slice.8
  278.8 18.3 %fusion.15 = bf16[32,512,256]{1,2,0:T(8,128)(2,1)} fusion(bf16[256,32,512]{2,1,0:T(8,128)(2,1)} %bitcast.10, bf16[32,256,256]{2,1,0:T(8,128)(2,1)} %param.11, bf16[]{:T(256)} %bitcast.11), kind=kOutput, calls=%fused_computation.19 | convolution fusion | flops 2160066560 | bytes 20971522 | tf_op jit(solution)/shard_map/pba,apd->bpd/dot_general | solution.py:137
  297.1 12.1 %copy.47 = bf16[8,32,32,512]{3,2,1,0:T(8,128)(2,1)} copy(bf16[8,32,32,512]{3,1,0,2:T(8,128)(2,1)} %bitcast.90) | data formatting | bytes 16777216 | tf_op jit(solution)/shard_map/reshape | solution.py:118
  309.2 44.4 %all-to-all-done.1 = bf16[8,32,32,512]{3,1,2,0:T(8,128)(2,1)} async-done(((bf16[8,32,32,512]{3,1,2,0:T(8,128)(2,1)}), bf16[8,32,32,512]{3,1,2,0:T(8,128)(2,1)}, u32[]{:S(2)}, u32[]{:S(2)}) %all-to-all-start.1) | async-done | bytes 8388640 | tf_op jit(solution)/shard_map/all_to_all | solution.py:112
  353.6 5.0 all-to-all-start.3
  359.3 11.7 %copy.42 = bf16[32,8,32,512]{3,2,1,0:T(8,128)(2,1)} copy(bf16[32,8,32,512]{3,0,2,1:T(8,128)(2,1)} %bitcast.5) | data formatting | bytes 16777216 | tf_op jit(solution)/shard_map/transpose | solution.py:119
  371.0 10.2 %multiply_convert_fusion.1 = bf16[32,256,256]{2,1,0:T(8,128)(2,1)} fusion(bf16[32,256,512]{2,1,0:T(8,128)(2,1)} %bitcast.88, bf16[32,256,512]{2,1,0:T(8,128)(2,1)} %bitcast.92), kind=kOutput, calls=%fused_computation.9 | convolution fusion | flops 2151677952 | bytes 20971520 | tf_op jit(solution)/shard_map/aqd,apd->aqp/dot_general | solution.py:141
  381.1 3.6 dynamic-slice_bitcast_fusion.2
  384.7 2.4 collective-permute-start
  387.1 2.6 collective-permute-start.1
  389.7 1.3 collective-permute-start.2
  391.0 6.3 convolution_convert_fusion.1
  397.3 11.1 %convolution_bitcast_fusion = f32[512,512]{1,0:T(8,128)} fusion(bf16[8192,512]{1,0:T(8,128)(2,1)S(1)} %bitcast.85, bf16[1,8192,512]{2,1,0:T(8,128)(2,1)} %param.6), kind=kOutput, calls=%fused_computation.33 | convolution fusion | flops 4294967296 | bytes 17825792 | tf_op jit(solution)/shard_map/dot_general | solution.py:152
  408.4 27.5 %collective-permute-done = bf16[8,256,256]{2,1,0:T(8,128)(2,1)} collective-permute-done((bf16[8,256,256]{2,1,0:T(8,128)(2,1)}, bf16[8,256,256]{2,1,0:T(8,128)(2,1)}, u32[]{:S(2)}, u32[]{:S(2)}) %collective-permute-start) | collective-permute-done | bytes 1048608 | tf_op jit(solution)/shard_map/ppermute | solution.py:73
  435.9 69.8 %collective-permute-done.1 = bf16[8,256,256]{2,1,0:T(8,128)(2,1)} collective-permute-done((bf16[8,256,256]{2,1,0:T(8,128)(2,1)}, bf16[8,256,256]{2,1,0:T(8,128)(2,1)}, u32[]{:S(2)}, u32[]{:S(2)}) %collective-permute-start.1) | collective-permute-done | bytes 1048608 | tf_op jit(solution)/shard_map/ppermute | solution.py:73
  505.7 4.4 broadcast_in_dim.28
  510.0 4.1 convert_dynamic-update-slice_fusion.3
  514.1 1.0 copy-done.3
  516.3 12.3 %convert_add_fusion = f32[8,32,32,512]{3,2,0,1:T(8,128)} fusion(bf16[8,32,32,512]{3,2,1,0:T(8,128)(2,1)} %all-to-all-done.3, f32[]{:T(128)S(6)} %convert.7), kind=kLoop, calls=%fused_computation.4 | loop fusion | flops 8388608 | bytes 25165828 | tf_op jit(solution)/shard_map/add | solution.py:154
  528.6 13.9 %fusion.27 = f32[512,512]{1,0:T(8,128)S(1)} fusion(f32[1,8192,512]{2,1,0:T(8,128)} %bitcast.82, bf16[1,8192,512]{2,1,0:T(8,128)(2,1)} %param.7, bf16[1,8192,512]{2,1,0:T(8,128)(2,1)} %param.6), kind=kOutput, calls=%fused_computation.32 | convolution fusion | flops 4307550208 | bytes 34603008 | tf_op jit(solution)/shard_map/dot_general | solution.py:155
  542.5 1.6 maximum_multiply_fusion
  544.1 3.6 all-to-all-start.4
  547.7 49.3 %collective-permute-start.3 = (bf16[8,256,256]{2,1,0:T(8,128)(2,1)}, bf16[8,256,256]{2,1,0:T(8,128)(2,1)}, u32[]{:S(2)}, u32[]{:S(2)}) collective-permute-start(bf16[8,256,256]{2,1,0:T(8,128)(2,1)} %copy-done.3), channel_id=1, source_target_pairs={{0,8},{8,16},{16,24},{24,0},{1,9},{9,17},{17,25},{25,1},{2,10},{10... | collective-permute-start | bytes 3145736 | tf_op jit(solution)/shard_map/ppermute | solution.py:73
  597.0 4.6 collective-permute-start.4
  601.6 0.9 reduce_sum.18
  602.6 12.0 %fusion.35 = f32[8192,512]{1,0:T(8,128)} fusion(bf16[8192,512]{1,0:T(8,128)(2,1)} %bitcast.86, bf16[512,512]{1,0:T(8,128)(2,1)S(1)} %copy-done), kind=kOutput, calls=%fused_computation.41 | convolution fusion | flops 4294967296 | bytes 25690112 | tf_op jit(solution)/shard_map/dot_general | solution.py:158
  614.6 11.0 %collective-permute-done.3 = bf16[8,256,256]{2,1,0:T(8,128)(2,1)} collective-permute-done((bf16[8,256,256]{2,1,0:T(8,128)(2,1)}, bf16[8,256,256]{2,1,0:T(8,128)(2,1)}, u32[]{:S(2)}, u32[]{:S(2)}) %collective-permute-start.3) | collective-permute-done | bytes 1048608 | tf_op jit(solution)/shard_map/ppermute | solution.py:73
  625.5 2.7 convert_dynamic-update-slice_fusion.2
  628.3 57.4 %collective-permute-done.4 = bf16[8,256,256]{2,1,0:T(8,128)(2,1)} collective-permute-done((bf16[8,256,256]{2,1,0:T(8,128)(2,1)}, bf16[8,256,256]{2,1,0:T(8,128)(2,1)}, u32[]{:S(2)}, u32[]{:S(2)}) %collective-permute-start.4) | collective-permute-done | bytes 1048608 | tf_op jit(solution)/shard_map/ppermute | solution.py:73
  685.6 2.7 convert_dynamic-update-slice_fusion.1
  688.4 2.7 convert_dynamic-update-slice_fusion
  691.1 6.6 convert_element_type.113
  697.8 2.0 reduce_sum.19
  699.8 12.0 %fusion = bf16[8192,512]{1,0:T(8,128)(2,1)} fusion(f32[8,32,32,512]{3,2,0,1:T(8,128)} %convert_add_fusion, bf16[1,8192,512]{2,1,0:T(8,128)(2,1)} %param.7), kind=kLoop, calls=%fused_computation.1 | loop fusion | flops 12582912 | bytes 33554432 | tf_op jit(solution)/shard_map/convert_element_type | solution.py:154
  711.9 12.6 %fusion.1 = bf16[1,8192,512]{2,1,0:T(8,128)(2,1)} fusion(f32[8192,512]{1,0:T(8,128)} %fusion.35, bf16[8192,512]{1,0:T(8,128)(2,1)} %fusion, bf16[512,512]{1,0:T(8,128)(2,1)S(1)} %copy-done.4), kind=kOutput, calls=%fused_computation.6 | convolution fusion | flops 4303355904 | bytes 34078720 | tf_op jit(solution)/shard_map/dot_general | solution.py:159
  724.4 23.2 %all-gather.4.cloned.1.call-done = f32[1024,512]{1,0:T(8,128)} async-done(((f32[128,512]{1,0:T(8,128)}), f32[1024,512]{1,0:T(8,128)}) %all-gather.4.cloned.1.call-update) | async-done | bytes 2097168 | tf_op jit(solution)/shard_map/all_gather | solution.py:99
  747.6 3.0 fusion.34
  (23 shorter events, 1.3 us)
Async XLA Ops:
  7.2 30.3 %copy-start = (bf16[512,512]{1,0:T(8,128)(2,1)S(1)}, bf16[512,512]{1,0:T(8,128)(2,1)}, u32[]{:S(2)}) copy-start(bf16[512,512]{1,0:T(8,128)(2,1)} %param.8) | copy-start | bytes 1572868
  32.3 99.7 %all-to-all-start = ((bf16[8,32,32,512]{3,2,1,0:T(8,128)(2,1)}), bf16[8,32,32,512]{3,2,1,0:T(8,128)(2,1)}, u32[]{:S(2)}, u32[]{:S(2)}) async-start(bf16[8,32,32,512]{3,2,1,0:T(8,128)(2,1)} %shard_map.101), calls=%async_computation | async-start | bytes 16777216 | tf_op jit(solution)/shard_map/all_to_all | solution.py:112
  155.4 99.0 %all-to-all-start.2 = ((bf16[8,32,32,512]{3,2,1,0:T(8,128)(2,1)}), bf16[8,32,32,512]{3,2,1,0:T(8,128)(2,1)}, u32[]{:S(2)}, u32[]{:S(2)}) async-start(bf16[8,32,32,512]{3,2,1,0:T(8,128)(2,1)} %shard_map.102), calls=%async_computation.2 | async-start | bytes 16777216 | tf_op jit(solution)/shard_map/all_to_all | solution.py:112
  254.5 99.1 %all-to-all-start.1 = ((bf16[8,32,32,512]{3,1,2,0:T(8,128)(2,1)}), bf16[8,32,32,512]{3,1,2,0:T(8,128)(2,1)}, u32[]{:S(2)}, u32[]{:S(2)}) async-start(bf16[8,32,32,512]{3,1,2,0:T(8,128)(2,1)} %copy.41), calls=%async_computation.1 | async-start | bytes 16777216 | tf_op jit(solution)/shard_map/all_to_all | solution.py:112
  353.6 162.7 %all-to-all-start.3 = ((bf16[8,32,32,512]{3,2,1,0:T(8,128)(2,1)}), bf16[8,32,32,512]{3,2,1,0:T(8,128)(2,1)}, u32[]{:S(2)}, u32[]{:S(2)}) async-start(bf16[8,32,32,512]{3,2,1,0:T(8,128)(2,1)} %copy.47), calls=%async_computation.3 | async-start | bytes 16777216 | tf_op jit(solution)/shard_map/all_to_all | solution.py:112
  358.5 332.6 %all-reduce.2.cloned.1.call-start = ((), (), s32[]{:S(2)}) async-start(), calls=%async_computation.6 | async-start | bytes 8388608 | tf_op jit(solution)/shard_map/psum | solution.py:139
  384.7 51.2 %collective-permute-start = (bf16[8,256,256]{2,1,0:T(8,128)(2,1)}, bf16[8,256,256]{2,1,0:T(8,128)(2,1)}, u32[]{:S(2)}, u32[]{:S(2)}) collective-permute-start(bf16[8,256,256]{2,1,0:T(8,128)(2,1)} %get-tuple-element.7), channel_id=1, source_target_pairs={{0,8},{8,16},{16,24},{24,0},{1,9},{9,17},{17,25},{25,1},{2,10},{10... | collective-permute-start | bytes 3145736 | tf_op jit(solution)/shard_map/ppermute | solution.py:73
  387.1 118.6 %collective-permute-start.1 = (bf16[8,256,256]{2,1,0:T(8,128)(2,1)}, bf16[8,256,256]{2,1,0:T(8,128)(2,1)}, u32[]{:S(2)}, u32[]{:S(2)}) collective-permute-start(bf16[8,256,256]{2,1,0:T(8,128)(2,1)} %get-tuple-element.9), channel_id=1, source_target_pairs={{0,16},{8,24},{16,0},{24,8},{1,17},{9,25},{17,1},{25,9},{2,18},{10... | collective-permute-start | bytes 3145736 | tf_op jit(solution)/shard_map/ppermute | solution.py:73
  389.7 116.0 %collective-permute-start.2 = (bf16[8,256,256]{2,1,0:T(8,128)(2,1)}, bf16[8,256,256]{2,1,0:T(8,128)(2,1)}, u32[]{:S(2)}, u32[]{:S(2)}) collective-permute-start(bf16[8,256,256]{2,1,0:T(8,128)(2,1)} %get-tuple-element.8), channel_id=1, source_target_pairs={{0,24},{8,0},{16,8},{24,16},{1,25},{9,1},{17,9},{25,17},{2,26},{10... | collective-permute-start | bytes 3145736 | tf_op jit(solution)/shard_map/ppermute | solution.py:73
  397.3 11.1 %copy-start.1 = (bf16[32,512,256]{1,2,0:T(8,128)(2,1)}, bf16[32,512,256]{1,2,0:T(8,128)(2,1)S(1)}, u32[]{:S(2)}) copy-start(bf16[32,512,256]{1,2,0:T(8,128)(2,1)S(1)} %convolution_convert_fusion.1) | copy-start | bytes 25165828
  514.1 1.0 copy-start.3
  528.6 13.9 %copy-start.2 = (f32[512,512]{1,0:T(8,128)S(1)}, f32[512,512]{1,0:T(8,128)}, u32[]{:S(2)}) copy-start(f32[512,512]{1,0:T(8,128)} %convolution_bitcast_fusion) | copy-start | bytes 3145732
  544.1 57.6 %all-to-all-start.4 = ((f32[8,128,512]{2,1,0:T(8,128)}), f32[8,128,512]{2,1,0:T(8,128)S(1)}, u32[]{:S(2)}, u32[]{:S(2)}) async-start(f32[8,128,512]{2,1,0:T(8,128)} %bitcast.93), calls=%async_computation.4 | async-start | bytes 4194304 | tf_op jit(solution)/shard_map/all_to_all | solution.py:94
  547.7 150.1 %all-gather.6.cloned.1.call-start = ((), (), s32[]{:S(2)}) async-start(), calls=%async_computation.7 | async-start | bytes 1310720 | tf_op jit(solution)/shard_map/all_gather | solution.py:98
  547.7 77.8 %collective-permute-start.3 = (bf16[8,256,256]{2,1,0:T(8,128)(2,1)}, bf16[8,256,256]{2,1,0:T(8,128)(2,1)}, u32[]{:S(2)}, u32[]{:S(2)}) collective-permute-start(bf16[8,256,256]{2,1,0:T(8,128)(2,1)} %copy-done.3), channel_id=1, source_target_pairs={{0,8},{8,16},{16,24},{24,0},{1,9},{9,17},{17,25},{25,1},{2,10},{10... | collective-permute-start | bytes 3145736 | tf_op jit(solution)/shard_map/ppermute | solution.py:73
  597.0 88.7 %collective-permute-start.4 = (bf16[8,256,256]{2,1,0:T(8,128)(2,1)}, bf16[8,256,256]{2,1,0:T(8,128)(2,1)}, u32[]{:S(2)}, u32[]{:S(2)}) collective-permute-start(bf16[8,256,256]{2,1,0:T(8,128)(2,1)} %copy-done.3), channel_id=1, source_target_pairs={{0,16},{8,24},{16,0},{24,8},{1,17},{9,25},{17,1},{25,9},{2,18},{10... | collective-permute-start | bytes 3145736 | tf_op jit(solution)/shard_map/ppermute | solution.py:73
  601.6 86.8 %collective-permute-start.5 = (bf16[8,256,256]{2,1,0:T(8,128)(2,1)}, bf16[8,256,256]{2,1,0:T(8,128)(2,1)}, u32[]{:S(2)}, u32[]{:S(2)}) collective-permute-start(bf16[8,256,256]{2,1,0:T(8,128)(2,1)} %copy-done.3), channel_id=1, source_target_pairs={{0,24},{8,0},{16,8},{24,16},{1,25},{9,1},{17,9},{25,17},{2,26},{10... | collective-permute-start | bytes 3145736 | tf_op jit(solution)/shard_map/ppermute | solution.py:73
  602.6 145.1 %all-gather.4.cloned.1.call-start = ((), (), s32[]{:S(2)}) async-start(), calls=%async_computation.5 | async-start | bytes 2359296 | tf_op jit(solution)/shard_map/all_gather | solution.py:99
  699.8 12.1 %copy-start.4 = (bf16[512,512]{1,0:T(8,128)(2,1)S(1)}, bf16[512,512]{1,0:T(8,128)(2,1)}, u32[]{:S(2)}) copy-start(bf16[512,512]{1,0:T(8,128)(2,1)} %w_ref.1) | copy-start | bytes 1572868
Sparse Core Ops, SparseCore 0:
  361.7 235.8 all-reduce.1
  602.7 83.8 all-gather.5
  699.9 47.6 all-gather.3
